TPU v7x, 32 devices: a whole 2x2x4 slice. The times are simulated.
32 devices in a mesh: wall: 8 (over z, y), span: 4 (over x, core).
Axes of the slice: x: 2, y: 2, z: 4, core: 2. Of those that a mesh axis runs over, the one named last changes fastest.
Arguments:
- random_planes: float32 [8, 3, 128, 4096], P(None, None, 'wall', 'span'), may hold values from -6 to 6
- previous: float32 [3, 128, 4096], P(None, 'wall', 'span'), may hold values from -6 to 6
- half_width: int32 [128], P('wall'), may hold values from 1 to 32
- time_scale: float32 [3, 128], P(None, 'wall'), may hold values from 1 to 16
- lund_factor: float32 [6, 128], P(None, 'wall'), may hold values from -4 to 4
- mean_velocity: float32 [128], P('wall'), may hold values from 0.5 to 1.5
Outputs:
- velocity: float32 [8, 3, 128, 4096], P(None, None, 'wall', 'span')
- filter_state: float32 [3, 128, 4096], P(None, 'wall', 'span')
All inputs are finite; a program needn't handle non-finite values.
Results may differ from a plain program's by a relative error of at most 0.000064.
Values sent between devices are 32-bit elements; how exact they have to be, the bound alone decides.
A program may use at most 128 MiB of HBM per device.

v0:
```python
import math

import jax
import jax.numpy as jnp
from jax import lax
from jax.sharding import PartitionSpec as P

HMAX = 32
HZ = 24


def shifted(shard, axis, by):
    length = lax.axis_size(axis)
    pairs = [(i, i + by) for i in range(length) if 0 <= i + by < length]
    return lax.ppermute(shard, axis, pairs)


def with_halo(block, sides, width):
    for axis, dim in sides:
        count = lax.axis_size(axis)
        forward = [(i, i + 1) for i in range(count - 1)]
        forward.append((count - 1, 0))
        backward = [(target, source) for source, target in forward]
        low = lax.ppermute(
            lax.slice_in_dim(block, block.shape[dim] - width, None, axis=dim), axis, forward
        )
        high = lax.ppermute(lax.slice_in_dim(block, 0, width, axis=dim), axis, backward)
        block = jnp.concatenate([low, block, high], axis=dim)
    return block


def band_matrix(widths, reach):
    height = widths.shape[0]
    row_index = lax.broadcasted_iota(jnp.int32, (height, height + 2 * reach), 0)
    column_index = lax.broadcasted_iota(jnp.int32, (height, height + 2 * reach), 1)
    offset = column_index - row_index - reach
    spread = widths.astype(jnp.float32)[:, None]
    distance = offset.astype(jnp.float32)
    shaped = jnp.where(
        jnp.abs(offset) <= widths[:, None],
        jnp.exp(-2.0 * math.pi * distance * distance / (spread * spread)),
        0.0,
    )
    return shaped / jnp.sqrt(jnp.sum(shaped * shaped, axis=1, keepdims=True))


def shards(random_planes, previous, half_width, time_scale, lund_factor, mean_velocity):
    highest = lax.Precision.HIGHEST
    row_count = random_planes.shape[2]
    depth = -(-HMAX // row_count)
    lower_parts = []
    upper_parts = []
    for distance in range(1, depth + 1):
        lower_parts.insert(0, shifted(random_planes, "wall", distance))
        upper_parts.append(shifted(random_planes, "wall", -distance))
    extended = jnp.concatenate(lower_parts + [random_planes] + upper_parts, axis=2)
    wall_band = band_matrix(half_width, HMAX)
    wall_pass = jnp.einsum("ik,sckz->sciz", wall_band, extended, precision=highest)
    margin = with_halo(wall_pass, (("span", 3),), HZ)
    layout = wall_pass.shape
    flat_margin = margin.reshape(-1, margin.shape[3])
    span_band = band_matrix(jnp.full((layout[3],), HZ, jnp.int32), HZ)
    filtered = jnp.einsum("rk,zk->rz", flat_margin, span_band, precision=highest).reshape(layout)
    retain = jnp.exp(-math.pi / (2.0 * time_scale))[:, :, None]
    inject = jnp.sqrt(1.0 - jnp.exp(-math.pi / time_scale))[:, :, None]
    factor = lund_factor[:, :, None]
    current = previous
    velocities = []
    for instant in range(filtered.shape[0]):
        current = retain * current + inject * filtered[instant]
        stream = mean_velocity[:, None] + factor[0] * current[0]
        normal = factor[1] * current[0] + factor[2] * current[1]
        spanwise = factor[3] * current[0] + factor[4] * current[1] + factor[5] * current[2]
        velocities.append(jnp.stack([stream, normal, spanwise]))
    return (jnp.stack(velocities), current)


def solution(mesh):
    in_specs = (
        P(None, None, "wall", "span"),
        P(None, "wall", "span"),
        P("wall"),
        P(None, "wall"),
        P(None, "wall"),
        P("wall"),
    )
    out_specs = (P(None, None, "wall", "span"), P(None, "wall", "span"))
    return jax.shard_map(shards, mesh=mesh, in_specs=in_specs, out_specs=out_specs, check_vma=False)
```

profile of v0, /device:TPU:0, one launch (start us, length us, event | category | flops | bytes accessed | tf_op | source)
XLA Modules:
  0.0 104.7 jit_solution(11685653262646541331)
XLA Ops:
  0.6 5.2 %collective-permute-start = (f32[8,3,16,1024]{3,2,1,0:T(8,128)}, f32[8,3,16,1024]{3,2,1,0:T(8,128)S(1)}, u32[]{:S(2)}, u32[]{:S(2)}) collective-permute-start(f32[8,3,16,1024]{3,2,1,0:T(8,128)} %param.6), channel_id=1, source_target_pairs={{0,8},{4,12},{8,16},{12,20},{16,24},{20,28},{1,9},{5,13},{9,17},{1... | collective-permute-start | bytes 4718600 | tf_op jit(solution)/shard_map/ppermute | solution.py:15
  5.8 3.5 %collective-permute-start.1 = (f32[8,3,16,1024]{3,2,1,0:T(8,128)}, f32[8,3,16,1024]{3,2,1,0:T(8,128)S(1)}, u32[]{:S(2)}, u32[]{:S(2)}) collective-permute-start(f32[8,3,16,1024]{3,2,1,0:T(8,128)} %param.6), channel_id=1, source_target_pairs={{0,4},{4,8},{8,12},{12,16},{16,20},{20,24},{24,28},{1,5},{5,9},{9,... | collective-permute-start | bytes 4718600 | tf_op jit(solution)/shard_map/ppermute | solution.py:15
  9.4 1.3 %collective-permute-start.2 = (f32[8,3,16,1024]{3,2,1,0:T(8,128)}, f32[8,3,16,1024]{3,2,1,0:T(8,128)S(1)}, u32[]{:S(2)}, u32[]{:S(2)}) collective-permute-start(f32[8,3,16,1024]{3,2,1,0:T(8,128)} %param.6), channel_id=1, source_target_pairs={{4,0},{8,4},{12,8},{16,12},{20,16},{24,20},{28,24},{5,1},{9,5},{13... | collective-permute-start | bytes 4718600 | tf_op jit(solution)/shard_map/ppermute | solution.py:15
  10.7 1.3 %collective-permute-start.3 = (f32[8,3,16,1024]{3,2,1,0:T(8,128)}, f32[8,3,16,1024]{3,2,1,0:T(8,128)S(1)}, u32[]{:S(2)}, u32[]{:S(2)}) collective-permute-start(f32[8,3,16,1024]{3,2,1,0:T(8,128)} %param.6), channel_id=1, source_target_pairs={{8,0},{12,4},{16,8},{20,12},{24,16},{28,20},{9,1},{13,5},{17,9},{2... | collective-permute-start | bytes 4718600 | tf_op jit(solution)/shard_map/ppermute | solution.py:15
  12.0 0.7 convert_multiply_fusion
  12.6 0.8 multiply_reduce_fusion.1
  13.5 1.5 %slice_bitcast_fusion.5 = (f32[16]{0:T(128)S(1)}, f32[16]{0:T(128)S(1)}, f32[16]{0:T(128)S(1)}, f32[16]{0:T(128)S(1)}, f32[16]{0:T(128)}, /*index=5*/f32[16]{0:T(128)}) fusion(f32[6,16]{1,0:T(8,128)} %param.10), kind=kLoop, calls=%fused_computation.93 | loop fusion | bytes 768 | tf_op jit(solution)/shard_map/slice | solution.py:71
  15.0 1.2 %multiply_reduce_fusion = f32[1024]{0:T(1024)S(1)} fusion(), kind=kLoop, calls=%fused_computation.6 | loop fusion | flops 12073984 | bytes 4096 | tf_op jit(solution)/shard_map/reduce_sum | solution.py:44
  16.2 23.5 %collective-permute-done = f32[8,3,16,1024]{3,2,1,0:T(8,128)S(1)} collective-permute-done((f32[8,3,16,1024]{3,2,1,0:T(8,128)}, f32[8,3,16,1024]{3,2,1,0:T(8,128)S(1)}, u32[]{:S(2)}, u32[]{:S(2)}) %collective-permute-start) | collective-permute-done | bytes 1572896 | tf_op jit(solution)/shard_map/ppermute | solution.py:15
  39.7 0.1 constant_dynamic-update-slice_fusion.4
  39.8 36.9 %collective-permute-done.1 = f32[8,3,16,1024]{3,2,1,0:T(8,128)S(1)} collective-permute-done((f32[8,3,16,1024]{3,2,1,0:T(8,128)}, f32[8,3,16,1024]{3,2,1,0:T(8,128)S(1)}, u32[]{:S(2)}, u32[]{:S(2)}) %collective-permute-start.1) | collective-permute-done | bytes 1572896 | tf_op jit(solution)/shard_map/ppermute | solution.py:15
  76.6 0.1 constant_dynamic-update-slice_fusion.3
  76.8 0.0 copy-done
  76.8 0.0 copy-start.10
  76.8 0.1 constant_dynamic-update-slice_fusion.2
  76.9 0.0 collective-permute-done.2
  76.9 0.1 constant_dynamic-update-slice_fusion.1
  77.0 4.5 %collective-permute-done.3 = f32[8,3,16,1024]{3,2,1,0:T(8,128)S(1)} collective-permute-done((f32[8,3,16,1024]{3,2,1,0:T(8,128)}, f32[8,3,16,1024]{3,2,1,0:T(8,128)S(1)}, u32[]{:S(2)}, u32[]{:S(2)}) %collective-permute-start.3) | collective-permute-done | bytes 1572896 | tf_op jit(solution)/shard_map/ppermute | solution.py:15
  81.6 0.1 constant_dynamic-update-slice_fusion
  81.7 0.0 copy-done.10
  81.7 0.0 copy-start.9
  81.7 4.1 %convolution_bitcast_fusion = f32[8,3,16,1024]{3,2,1,0:T(8,128)S(1)} fusion(f32[8,3,80,1024]{3,2,1,0:T(8,128)S(1)} %constant_dynamic-update-slice_fusion, f32[16]{0:T(128)S(1)} %sqrt.20, f32[16]{0:T(128)S(1)} %convert_multiply_fusion, s32[16]{0:T(128)S(1)} %copy-done.10), kind=kOutput, calls=%fused_computation.14 | convolution fusion | flops 377500160 | bytes 9437376 | tf_op jit(solution)/shard_map/ik,sckz->sciz/dot_general | solution.py:58
  85.8 0.1 fusion.44
  86.0 0.1 collective-permute-start.4
  86.0 1.7 %collective-permute-start.5 = (f32[8,3,16,24]{3,2,1,0:T(8,128)S(1)}, f32[8,3,16,24]{3,2,1,0:T(8,128)}, u32[]{:S(2)}, u32[]{:S(2)}) collective-permute-start(f32[8,3,16,24]{3,2,1,0:T(8,128)S(1)} %get-tuple-element.18), channel_id=1, source_target_pairs={{1,0},{2,1},{3,2},{0,3},{5,4},{6,5},{7,6},{4,7},{9,8},{10,9},{11,1... | collective-permute-start | bytes 110600 | tf_op jit(solution)/shard_map/ppermute | solution.py:27
  87.8 0.6 divide_exponential_fusion
  88.4 0.6 sqrt.21
  89.0 2.5 %collective-permute-done.4 = f32[8,3,16,24]{3,2,1,0:T(8,128)S(1)} collective-permute-done((f32[8,3,16,24]{3,2,1,0:T(8,128)S(1)}, f32[8,3,16,24]{3,2,1,0:T(8,128)S(1)}, u32[]{:S(2)}, u32[]{:S(2)}) %collective-permute-start.4) | collective-permute-done | bytes 36896 | tf_op jit(solution)/shard_map/ppermute | solution.py:24
  91.4 0.8 collective-permute-done.5
  92.2 1.9 %concatenate.7 = f32[8,3,16,1072]{3,2,1,0:T(8,128)S(1)} concatenate(f32[8,3,16,24]{3,2,1,0:T(8,128)S(1)} %collective-permute-done.4, f32[8,3,16,1024]{3,2,1,0:T(8,128)S(1)} %convolution_bitcast_fusion, f32[8,3,16,24]{3,2,1,0:T(8,128)} %collective-permute-done.5), dimensions={3} | concatenate | bytes 3293184 | tf_op jit(solution)/shard_map/concatenate | solution.py:28
  94.2 0.0 copy-start.2
  94.2 0.0 copy-start.6
  94.2 8.0 %fusion.3 = f32[384,1024]{1,0:T(8,128)S(1)} fusion(f32[384,1072]{1,0:T(8,128)S(1)} %bitcast.62, f32[1024]{0:T(1024)} %sqrt.21), kind=kOutput, calls=%fused_computation.4 | convolution fusion | flops 5069307904 | bytes 3223552 | tf_op jit(solution)/shard_map/rk,zk->rz/dot_general | solution.py:63
  102.2 0.0 copy-start.4
  102.2 0.0 copy-start.5
  102.2 0.0 copy-start.8
  102.2 0.1 fusion.43
  102.3 0.0 copy-done.2
  102.4 0.3 multiply_add_fusion
  102.7 0.0 copy-start.1
  102.7 0.2 copy-done.4
  102.9 0.0 copy-done.8
  102.9 0.1 multiply_add_fusion.23
  103.0 0.1 multiply_add_fusion.21
  103.1 0.1 multiply_add_fusion.19
  103.3 0.1 multiply_add_fusion.17
  103.6 0.0 copy-start.3
  103.6 1.1 %copy-done.3 = f32[8,3,16,1024]{3,2,1,0:T(8,128)} copy-done((f32[8,3,16,1024]{3,2,1,0:T(8,128)}, f32[8,3,16,1024]{3,2,1,0:T(8,128)S(1)}, u32[]{:S(2)}) %copy-start.3) | copy-done | bytes 1572888
  (16 shorter events, 0.2 us)
Async XLA Ops:
  0.6 76.1 %copy-start = (f32[8,3,16,1024]{3,2,1,0:T(8,128)S(1)}, f32[8,3,16,1024]{3,2,1,0:T(8,128)}, u32[]{:S(2)}) copy-start(f32[8,3,16,1024]{3,2,1,0:T(8,128)} %param.6) | copy-start | bytes 4718596
  0.6 39.0 %collective-permute-start = (f32[8,3,16,1024]{3,2,1,0:T(8,128)}, f32[8,3,16,1024]{3,2,1,0:T(8,128)S(1)}, u32[]{:S(2)}, u32[]{:S(2)}) collective-permute-start(f32[8,3,16,1024]{3,2,1,0:T(8,128)} %param.6), channel_id=1, source_target_pairs={{0,8},{4,12},{8,16},{12,20},{16,24},{20,28},{1,9},{5,13},{9,17},{1... | collective-permute-start | bytes 4718600 | tf_op jit(solution)/shard_map/ppermute | solution.py:15
  5.8 70.8 %collective-permute-start.1 = (f32[8,3,16,1024]{3,2,1,0:T(8,128)}, f32[8,3,16,1024]{3,2,1,0:T(8,128)S(1)}, u32[]{:S(2)}, u32[]{:S(2)}) collective-permute-start(f32[8,3,16,1024]{3,2,1,0:T(8,128)} %param.6), channel_id=1, source_target_pairs={{0,4},{4,8},{8,12},{12,16},{16,20},{20,24},{24,28},{1,5},{5,9},{9,... | collective-permute-start | bytes 4718600 | tf_op jit(solution)/shard_map/ppermute | solution.py:15
  9.4 67.5 %collective-permute-start.2 = (f32[8,3,16,1024]{3,2,1,0:T(8,128)}, f32[8,3,16,1024]{3,2,1,0:T(8,128)S(1)}, u32[]{:S(2)}, u32[]{:S(2)}) collective-permute-start(f32[8,3,16,1024]{3,2,1,0:T(8,128)} %param.6), channel_id=1, source_target_pairs={{4,0},{8,4},{12,8},{16,12},{20,16},{24,20},{28,24},{5,1},{9,5},{13... | collective-permute-start | bytes 4718600 | tf_op jit(solution)/shard_map/ppermute | solution.py:15
  10.7 70.9 %collective-permute-start.3 = (f32[8,3,16,1024]{3,2,1,0:T(8,128)}, f32[8,3,16,1024]{3,2,1,0:T(8,128)S(1)}, u32[]{:S(2)}, u32[]{:S(2)}) collective-permute-start(f32[8,3,16,1024]{3,2,1,0:T(8,128)} %param.6), channel_id=1, source_target_pairs={{8,0},{12,4},{16,8},{20,12},{24,16},{28,20},{9,1},{13,5},{17,9},{2... | collective-permute-start | bytes 4718600 | tf_op jit(solution)/shard_map/ppermute | solution.py:15
  76.8 4.9 %copy-start.10 = (s32[16]{0:T(128)S(1)}, s32[16]{0:T(128)}, u32[]{:S(2)}) copy-start(s32[16]{0:T(128)} %param.8) | copy-start | bytes 196
  81.7 6.1 %copy-start.9 = (f32[3,16]{1,0:T(4,128)S(1)}, f32[3,16]{1,0:T(4,128)}, u32[]{:S(2)}) copy-start(f32[3,16]{1,0:T(4,128)} %param.9) | copy-start | bytes 580
  86.0 5.5 %collective-permute-start.4 = (f32[8,3,16,24]{3,2,1,0:T(8,128)S(1)}, f32[8,3,16,24]{3,2,1,0:T(8,128)S(1)}, u32[]{:S(2)}, u32[]{:S(2)}) collective-permute-start(f32[8,3,16,24]{3,2,1,0:T(8,128)S(1)} %get-tuple-element.19), channel_id=1, source_target_pairs={{0,1},{1,2},{2,3},{3,0},{4,5},{5,6},{6,7},{7,4},{8,9},{9,10},{10,1... | collective-permute-start | bytes 110600 | tf_op jit(solution)/shard_map/ppermute | solution.py:24
  86.0 6.2 %collective-permute-start.5 = (f32[8,3,16,24]{3,2,1,0:T(8,128)S(1)}, f32[8,3,16,24]{3,2,1,0:T(8,128)}, u32[]{:S(2)}, u32[]{:S(2)}) collective-permute-start(f32[8,3,16,24]{3,2,1,0:T(8,128)S(1)} %get-tuple-element.18), channel_id=1, source_target_pairs={{1,0},{2,1},{3,2},{0,3},{5,4},{6,5},{7,6},{4,7},{9,8},{10,9},{11,1... | collective-permute-start | bytes 110600 | tf_op jit(solution)/shard_map/ppermute | solution.py:27
  94.2 8.2 %copy-start.2 = (f32[3,16,1024]{2,1,0:T(8,128)S(1)}, f32[3,16,1024]{2,1,0:T(8,128)}, u32[]{:S(2)}) copy-start(f32[3,16,1024]{2,1,0:T(8,128)} %param.7) | copy-start | bytes 589828
  94.2 8.2 %copy-start.6 = (f32[3,16]{1,0:T(4,128)S(1)}, f32[3,16]{1,0:T(4,128)}, u32[]{:S(2)}) copy-start(f32[3,16]{1,0:T(4,128)} %get-tuple-element.62) | copy-start | bytes 580
  94.2 8.2 %copy-start.7 = (f32[3,16]{1,0:T(4,128)S(1)}, f32[3,16]{1,0:T(4,128)}, u32[]{:S(2)}) copy-start(f32[3,16]{1,0:T(4,128)} %get-tuple-element.63) | copy-start | bytes 580
  102.2 0.7 copy-start.4
  102.2 0.7 copy-start.5
  102.2 0.7 copy-start.8
  102.7 0.9 copy-start.1
  103.6 1.1 %copy-start.3 = (f32[8,3,16,1024]{3,2,1,0:T(8,128)}, f32[8,3,16,1024]{3,2,1,0:T(8,128)S(1)}, u32[]{:S(2)}) copy-start(f32[8,3,16,1024]{3,2,1,0:T(8,128)S(1)} %fusion.19) | copy-start | bytes 4718596
where the time goes:
time: 105 us
  waiting for transfers between devices  68.2 us (65%)
  starting transfers between devices  13.1 us (12%)
  matrix products  12.1 us (12%)
  local copies, waits for them, and re-layouts  6.13 us (6%)
  other arithmetic  4.23 us (4%)
    ppermute x4, waiting for transfers between devices, shifted(): return lax.ppermute(shard, axis, pairs)  64.9 us
    ppermute x4, starting transfers between devices, shifted(): return lax.ppermute(shard, axis, pairs)  11.3 us
    dot_general x1, matrix products, shards(): jnp.einsum('rk,zk->rz', flat_margin, span_band, precision=highest)  7.99 us
    dot_general x1, matrix products, shards(): jnp.einsum('ik,sckz->sciz', wall_band, extended, precision=highest)  4.14 us
    ppermute x1, waiting for transfers between devices, with_halo(): lax.ppermute(lax.slice_in_dim(block, block.shape[dim] - width, None, axis...  2.45 us
  transfers between devices with their start and end apart: 6, of which 5 were waited for; matrix products, arithmetic and copies ran while one was open for 6% of the time, Pallas kernels for 0%

commit v1 on v0

v1 whole, which is shorter than its diff:
```python
import functools
import math

import jax
import jax.numpy as jnp
from jax import lax
from jax.experimental import pallas as pl
from jax.experimental.pallas import tpu as pltpu
from jax.sharding import PartitionSpec as P

HMAX = 32
HZ = 24
LANES = 128
MESH = pl.DeviceIdType.MESH
BF16 = jnp.bfloat16
F32 = jnp.float32

GATHER, UP_OWN, UP_FWD, DOWN_OWN, DOWN_FWD, RETURN, HALO_LEFT, HALO_RIGHT = range(8)
KINDS = 8


def halves(x):
    head = x.astype(BF16)
    return head, (x - head.astype(F32)).astype(BF16)


def columns_of(row):
    n = row.shape[1]
    diagonal = lax.broadcasted_iota(jnp.int32, (n, n), 0) == lax.broadcasted_iota(jnp.int32, (n, n), 1)
    return jnp.sum(jnp.where(diagonal, jnp.broadcast_to(row, (n, n)), 0.0), axis=1, keepdims=True)


def kernel(
    planes, previous, width, scale, lund, mean, velocity, state,
    ext, share, full, out, field, other_width, wall_w, span_head, span_rest,
    send, recv, local, drain, width_sem,
):
    steps, parts, rows, cells = planes.shape
    half = cells // 2
    pair_rows = 2 * rows
    reach = HMAX
    pairs = lax.axis_size("wall") // 2
    spans = lax.axis_size("span")
    wall = lax.axis_index("wall")
    span = lax.axis_index("span")
    pair = wall // 2
    side = wall % 2
    partner = wall + 1 - 2 * side
    right = (span + 1) % spans
    left = (span + spans - 1) % spans
    has_lower = pair > 0
    has_upper = pair < pairs - 1

    barrier = pltpu.get_barrier_semaphore()

    def greet(wall_at, span_at):
        pl.semaphore_signal(
            barrier, inc=1, device_id={"wall": wall_at, "span": span_at}, device_id_type=MESH
        )

    greet(partner, span)
    for beside in (left, right):
        greet(wall, beside)
        greet(partner, beside)

    @pl.when(has_lower)
    def _():
        greet(wall - 2, span)

    @pl.when(has_upper)
    def _():
        greet(wall + 2, span)

    own_rows = pl.ds(pl.multiple_of(rows * side, rows), rows)
    other_rows = pl.ds(pl.multiple_of(rows * (1 - side), rows), rows)
    own_mid = pl.ds(pl.multiple_of(reach + rows * side, rows), rows)
    other_mid = pl.ds(pl.multiple_of(reach + rows * (1 - side), rows), rows)
    own_top = pl.ds(pl.multiple_of(reach + pair_rows + rows * side, rows), rows)
    other_top = pl.ds(pl.multiple_of(reach + pair_rows + rows * (1 - side), rows), rows)
    own_half = pl.ds(pl.multiple_of(half * side, LANES), half)
    other_half = pl.ds(pl.multiple_of(half * (1 - side), LANES), half)
    own_cells = pl.ds(pl.multiple_of(LANES + half * side, LANES), half)
    other_cells = pl.ds(pl.multiple_of(LANES + half * (1 - side), LANES), half)
    edge_in_half = pl.ds(pl.multiple_of((half - LANES) * side, LANES), LANES)
    edge_in_full = pl.ds(pl.multiple_of(LANES + (cells - LANES) * side, LANES), LANES)
    halo_there = pl.ds(pl.multiple_of((LANES + cells) * (1 - side), LANES), LANES)
    toward = (span + spans + 2 * side - 1) % spans
    halo_kind = HALO_LEFT + 1 - side

    def remote(source, target, send_at, recv_at, wall_at, span_at):
        return pltpu.make_async_remote_copy(
            src_ref=source, dst_ref=target, send_sem=send.at[send_at], recv_sem=recv.at[recv_at],
            device_id={"wall": wall_at, "span": span_at}, device_id_type=MESH,
        )

    def gather(s):
        at = GATHER * steps + s
        return remote(planes.at[s, :, :, other_half], ext.at[s, :, own_mid, :], at, at, partner, span)

    def up_own(s):
        at = UP_OWN * steps + s
        return remote(planes.at[s, :, :, own_half], ext.at[s, :, own_rows, :], at, at, wall + 2, span)

    def up_fwd(s):
        at = UP_FWD * steps + s
        return remote(ext.at[s, :, other_mid, :], ext.at[s, :, other_rows, :], at, at, wall + 2, span)

    def down_own(s):
        at = DOWN_OWN * steps + s
        return remote(planes.at[s, :, :, own_half], ext.at[s, :, own_top, :], at, at, wall - 2, span)

    def down_fwd(s):
        at = DOWN_FWD * steps + s
        return remote(ext.at[s, :, other_mid, :], ext.at[s, :, other_top, :], at, at, wall - 2, span)

    def give_back(s):
        at = RETURN * steps + s
        return remote(share.at[s], full.at[s, :, :, own_cells], at, at, partner, span)

    def halo_partner(s):
        return remote(
            share.at[s, :, :, edge_in_half], full.at[s, :, :, halo_there],
            HALO_LEFT * steps + s, halo_kind * steps + s, partner, toward,
        )

    def halo_own(s):
        return remote(
            full.at[s, :, :, edge_in_full], full.at[s, :, :, halo_there],
            HALO_RIGHT * steps + s, halo_kind * steps + s, wall, toward,
        )

    def arrival(target, kind, s):
        at = kind * steps + s
        return remote(target, target, at, at, partner, span)

    own_in = [
        pltpu.make_async_copy(planes.at[s, :, :, own_half], ext.at[s, :, own_mid, :], local.at[s])
        for s in range(steps)
    ]
    field_in = pltpu.make_async_copy(previous, field, local.at[steps])
    width_out = pltpu.make_async_remote_copy(
        src_ref=width, dst_ref=other_width, send_sem=width_sem.at[0], recv_sem=width_sem.at[1],
        device_id={"wall": partner, "span": span}, device_id_type=MESH,
    )

    pl.semaphore_wait(barrier, 5 + has_lower.astype(jnp.int32) + has_upper.astype(jnp.int32))

    width_out.start()
    for s in range(steps):
        gather(s).start()

        @pl.when(has_upper)
        def _():
            up_own(s).start()

        @pl.when(has_lower)
        def _():
            down_own(s).start()

    field_in.start()
    for s in range(steps):
        own_in[s].start()

    @pl.when(pair == 0)
    def _():
        for s in range(steps):
            ext[s, :, 0:reach, :] = jnp.zeros((parts, reach, half), F32)

    @pl.when(pair == pairs - 1)
    def _():
        for s in range(steps):
            ext[s, :, reach + pair_rows:, :] = jnp.zeros((parts, reach, half), F32)

    tile = 2 * LANES
    depth = tile + 2 * LANES
    offset = (
        lax.broadcasted_iota(jnp.int32, (depth, tile), 0)
        - lax.broadcasted_iota(jnp.int32, (depth, tile), 1)
        - LANES
    )
    norm = math.sqrt(sum(math.exp(-2.0 * math.pi * j * j / (HZ * HZ)) ** 2 for j in range(-HZ, HZ + 1)))
    distance = offset.astype(F32)
    band = jnp.where(
        jnp.abs(offset) <= HZ, jnp.exp(distance * distance * (-2.0 * math.pi / (HZ * HZ))), 0.0
    ) * (1.0 / norm)
    head, rest = halves(band)
    span_head[...] = head
    span_rest[...] = rest

    retain_rows = jnp.exp(-math.pi / (2.0 * scale[...]))
    inject_rows = jnp.sqrt(1.0 - jnp.exp(-math.pi / scale[...]))
    retain = [columns_of(retain_rows[c:c + 1]) for c in range(parts)]
    inject = [columns_of(inject_rows[c:c + 1]) for c in range(parts)]
    factor = [columns_of(lund[i:i + 1, :]) for i in range(6)]
    drift = columns_of(mean[...])

    width_out.wait()
    depth_w = reach + pair_rows + reach
    lane = lax.broadcasted_iota(jnp.int32, (rows, 2 * depth_w), 1)
    line = lax.broadcasted_iota(jnp.int32, (rows, 2 * depth_w), 0)
    source = jnp.where(lane >= depth_w, lane - depth_w, lane)

    def wall_weights(widths, first):
        spread = columns_of(widths.astype(F32))
        apart = (source - reach - line - first).astype(F32)
        shaped = jnp.where(
            jnp.abs(apart) <= spread, jnp.exp(-2.0 * math.pi * apart * apart / (spread * spread)), 0.0
        )
        once = jnp.where(lane < depth_w, shaped * shaped, 0.0)
        return shaped / jnp.sqrt(jnp.sum(once, axis=1, keepdims=True))

    weights = jnp.concatenate(
        [wall_weights(width[...], rows * side), wall_weights(other_width[...], rows * (1 - side))], axis=0
    )
    head = weights.astype(BF16).astype(F32)
    first_copy = lax.broadcasted_iota(jnp.int32, weights.shape, 1) < depth_w
    wall_w[...] = jnp.concatenate([head, jnp.where(first_copy, weights - head, 0.0)], axis=0).astype(BF16)

    for s in range(steps):
        arrival(ext.at[s, :, other_mid, :], GATHER, s).wait_recv()

        @pl.when(has_upper)
        def _():
            up_fwd(s).start()

        @pl.when(has_lower)
        def _():
            down_fwd(s).start()

    field_in.wait()
    current = [field[c] for c in range(parts)]

    def finish(s, current):
        arrival(full.at[s, :, :, other_cells], RETURN, s).wait_recv()
        arrival(full.at[s, :, :, 0:LANES], HALO_LEFT, s).wait_recv()
        arrival(full.at[s, :, :, LANES + cells:], HALO_RIGHT, s).wait_recv()
        head, rest = halves(full[s].reshape(parts * rows, cells + 2 * LANES))
        tiles = cells // tile
        heads = jnp.concatenate([head[:, tile * t:tile * t + depth] for t in range(tiles)], axis=0)
        rests = jnp.concatenate([rest[:, tile * t:tile * t + depth] for t in range(tiles)], axis=0)
        count = heads.shape[0]
        both = jnp.dot(jnp.concatenate([heads, rests], axis=0), span_head[...], preferred_element_type=F32)
        low = jnp.dot(heads, span_rest[...], preferred_element_type=F32)
        total = both[:count] + both[count:] + low
        step = parts * rows
        filtered = jnp.concatenate([total[step * t:step * (t + 1)] for t in range(tiles)], axis=1)
        new = [
            retain[c] * current[c] + inject[c] * filtered[rows * c:rows * (c + 1)] for c in range(parts)
        ]
        out[s, 0] = drift + factor[0] * new[0]
        out[s, 1] = factor[1] * new[0] + factor[2] * new[1]
        out[s, 2] = factor[3] * new[0] + factor[4] * new[1] + factor[5] * new[2]
        pltpu.make_async_copy(out.at[s], velocity.at[s], drain.at[s]).start()
        return new

    for s in range(steps):
        own_in[s].wait()

        @pl.when(has_lower)
        def _():
            arrival(ext.at[s, :, own_rows, :], UP_OWN, s).wait_recv()
            arrival(ext.at[s, :, other_rows, :], UP_FWD, s).wait_recv()

        @pl.when(has_upper)
        def _():
            arrival(ext.at[s, :, own_top, :], DOWN_OWN, s).wait_recv()
            arrival(ext.at[s, :, other_top, :], DOWN_FWD, s).wait_recv()

        for c in range(parts):
            head, rest = halves(ext[s, c])
            made = jnp.dot(
                wall_w[...], jnp.concatenate([head, rest], axis=0), preferred_element_type=F32
            )
            passed = made[:pair_rows] + made[pair_rows:]
            share[s, c] = passed[rows:]
            full[s, c, :, own_cells] = passed[:rows]
        give_back(s).start()
        halo_partner(s).start()
        halo_own(s).start()
        if s > 0:
            current = finish(s - 1, current)
    current = finish(steps - 1, current)
    for c in range(parts):
        field[c] = current[c]
    state_out = pltpu.make_async_copy(field, state, drain.at[steps])
    state_out.start()

    for s in range(steps):
        gather(s).wait_send()
        give_back(s).wait_send()
        halo_partner(s).wait_send()
        halo_own(s).wait_send()

        @pl.when(has_upper)
        def _():
            up_own(s).wait_send()
            up_fwd(s).wait_send()

        @pl.when(has_lower)
        def _():
            down_own(s).wait_send()
            down_fwd(s).wait_send()

        pltpu.make_async_copy(out.at[s], velocity.at[s], drain.at[s]).wait()
    state_out.wait()


def shards(random_planes, previous, half_width, time_scale, lund_factor, mean_velocity):
    steps, parts, rows, cells = random_planes.shape
    pair_rows = 2 * rows
    assert pair_rows >= HMAX and lax.axis_size("wall") % 2 == 0
    depth = HMAX + pair_rows + HMAX
    any_space = pl.BlockSpec(memory_space=pl.ANY)
    vmem = pl.BlockSpec(memory_space=pltpu.VMEM)
    dma = pltpu.SemaphoreType.DMA
    return pl.pallas_call(
        kernel,
        out_shape=(
            jax.ShapeDtypeStruct(random_planes.shape, F32),
            jax.ShapeDtypeStruct(previous.shape, F32),
        ),
        in_specs=[any_space, any_space, vmem, vmem, vmem, vmem],
        out_specs=(any_space, any_space),
        scratch_shapes=[
            pltpu.VMEM((steps, parts, depth, cells // 2), F32),
            pltpu.VMEM((steps, parts, rows, cells // 2), F32),
            pltpu.VMEM((steps, parts, rows, cells + 2 * LANES), F32),
            pltpu.VMEM((steps, parts, rows, cells), F32),
            pltpu.VMEM((parts, rows, cells), F32),
            pltpu.VMEM((1, rows), jnp.int32),
            pltpu.VMEM((2 * pair_rows, 2 * depth), BF16),
            pltpu.VMEM((4 * LANES, 2 * LANES), BF16),
            pltpu.VMEM((4 * LANES, 2 * LANES), BF16),
            dma((KINDS * steps,)),
            dma((KINDS * steps,)),
            dma((steps + 1,)),
            dma((steps + 1,)),
            dma((2,)),
        ],
        compiler_params=pltpu.CompilerParams(collective_id=0, has_side_effects=True),
        name="inflow",
    )(
        random_planes, previous, half_width.reshape(1, rows), time_scale, lund_factor,
        mean_velocity.reshape(1, rows),
    )


def solution(mesh):
    in_specs = (
        P(None, None, "wall", "span"),
        P(None, "wall", "span"),
        P("wall"),
        P(None, "wall"),
        P(None, "wall"),
        P("wall"),
    )
    out_specs = (P(None, None, "wall", "span"), P(None, "wall", "span"))
    return jax.shard_map(shards, mesh=mesh, in_specs=in_specs, out_specs=out_specs, check_vma=False)
```

time: 105 us -> 57.5 us (0.55)
  waiting for transfers between devices: 68.2 us -> 0 us
  Pallas kernels: 0 us -> 53.3 us
  starting transfers between devices: 13.1 us -> 0 us
  matrix products: 12.1 us -> 0 us
  other arithmetic: 4.23 us -> 0 us
  local copies, waits for them, and re-layouts: 6.13 us -> 3.45 us
    ppermute x6 -> x0, waiting for transfers between devices: 68.2 us -> none  [the longest x4 64.9 us: shifted(): return lax.ppermute(shard, axis, pairs)]
    pallas_call x0 -> x1, Pallas kernels: none -> 53.3 us  [shards(): pl.pallas_call(kernel, out_shape=(jax.ShapeDtypeStruct(random_planes.shap...]
    ppermute x6 -> x0, starting transfers between devices: 13.1 us -> none  [the longest x4 11.3 us: shifted(): return lax.ppermute(shard, axis, pairs)]
    dot_general x2 -> x0, matrix products: 12.1 us -> none  [the longest x1 7.99 us: shards(): jnp.einsum('rk,zk->rz', flat_margin, span_band, precision=highest)]
    reduce_sum x2 -> x0, other arithmetic: 2.03 us -> none  [band_matrix(): return shaped / jnp.sqrt(jnp.sum(shaped * shaped, axis=1, keepdims=True))]
    concatenate x2 -> x0, local copies, waits for them, and re-layouts: 2.02 us -> none  [the longest x1 1.92 us: with_halo(): block = jnp.concatenate([low, block, high], axis=dim)]
    slice x3 -> x0, local copies, waits for them, and re-layouts: 1.73 us -> none  [the longest x1 1.5 us: shards(): stream = mean_velocity[:, None] + factor[0] * current[0]]
    unnamed x26 -> x4, local copies, waits for them, and re-layouts: 1.77 us -> 3.45 us
  transfers between devices with their start and end apart: 6 -> 0, of which waited for: 5 -> 0; matrix products, arithmetic and copies ran while one was open for 6% -> 0% of each run, Pallas kernels for 0% -> 0%
where the time goes in v1:
time: 57.5 us; the launch traced here: 57.4 us
  Pallas kernels  53.3 us (93%)
  local copies, waits for them, and re-layouts  3.45 us (6%)
  between operations  0.65 us (1%)
    pallas_call x1, Pallas kernels, shards(): pl.pallas_call(kernel, out_shape=(jax.ShapeDtypeStruct(random_planes.shap...  53.3 us
    unnamed x4, local copies, waits for them, and re-layouts  3.45 us

profile of v1, /device:TPU:0, one launch (start us, length us, event | category | flops | bytes accessed | tf_op | source)
XLA Modules:
  0.0 57.4 jit_solution(6386367038030706735)
XLA Ops:
  0.6 53.3 %inflow.1 = (f32[8,3,16,1024]{3,2,1,0:T(8,128)}, f32[3,16,1024]{2,1,0:T(8,128)}) custom-call(f32[8,3,16,1024]{3,2,1,0:T(8,128)} %planes.1, f32[3,16,1024]{2,1,0:T(8,128)} %previous.1, s32[1,16]{1,0:T(1,128)} %bitcast.2, f32[3,16]{1,0:T(4,128)} %scale.1, f32[6,16]{1,0:T(8,128)} %lund.1, f32[1,16]{1,0:T(1,128)} %bitcast.3), custom_call_target="tpu_custom_call" | custom-call | tf_op jit(solution)/shard_map/inflow/pallas_call | solution.py:316
  53.9 0.0 copy-start
  53.9 2.8 %copy.10 = f32[8,3,16,1024]{3,2,1,0:T(8,128)} copy(f32[8,3,16,1024]{3,2,1,0:T(8,128)} %get-tuple-element.4) | data formatting | bytes 3145728
  56.7 0.0 copy-done
  56.7 0.7 %copy.11 = f32[3,16,1024]{2,1,0:T(8,128)} copy(f32[3,16,1024]{2,1,0:T(8,128)S(1)} %copy-done) | data formatting | bytes 393216
Async XLA Ops:
  53.9 2.8 %copy-start = (f32[3,16,1024]{2,1,0:T(8,128)S(1)}, f32[3,16,1024]{2,1,0:T(8,128)}, u32[]{:S(2)}) copy-start(f32[3,16,1024]{2,1,0:T(8,128)} %get-tuple-element.5) | copy-start | bytes 589828

commit v2 on v1

v2 whole, which is shorter than its diff:
```python
import functools
import math

import jax
import jax.numpy as jnp
from jax import lax
from jax.experimental import pallas as pl
from jax.experimental.pallas import tpu as pltpu
from jax.sharding import PartitionSpec as P

HMAX = 32
HZ = 24
LANES = 128
MESH = pl.DeviceIdType.MESH
BF16 = jnp.bfloat16
F32 = jnp.float32

GATHER, UP_OWN, UP_FWD, DOWN_OWN, DOWN_FWD, RETURN, HALO_LEFT, HALO_RIGHT = range(8)
KINDS = 8
AHEAD = 2
LEAD = 4
VMEM_LIMIT = 24 * 2**20


def halves(x):
    head = x.astype(BF16)
    return head, (x - head.astype(F32)).astype(BF16)


def chunks_of(steps, parts):
    return [(s, 0, parts) for s in range(steps - 1)] + [(steps - 1, c, c + 1) for c in range(parts)]


def columns_of(row):
    n = row.shape[1]
    diagonal = lax.broadcasted_iota(jnp.int32, (n, n), 0) == lax.broadcasted_iota(jnp.int32, (n, n), 1)
    return jnp.sum(jnp.where(diagonal, jnp.broadcast_to(row, (n, n)), 0.0), axis=1, keepdims=True)


def kernel(
    planes, previous, width, scale, lund, mean, velocity, state,
    ext, share, full, field, other_width, wall_w, span_head, span_rest,
    send, recv, local, width_sem,
):
    steps, parts, rows, cells = planes.shape
    chunks = chunks_of(steps, parts)
    count = len(chunks)
    half = cells // 2
    pair_rows = 2 * rows
    reach = HMAX
    pairs = lax.axis_size("wall") // 2
    spans = lax.axis_size("span")
    wall = lax.axis_index("wall")
    span = lax.axis_index("span")
    pair = wall // 2
    side = wall % 2
    partner = wall + 1 - 2 * side
    right = (span + 1) % spans
    left = (span + spans - 1) % spans
    has_lower = pair > 0
    has_upper = pair < pairs - 1

    barrier = pltpu.get_barrier_semaphore()

    def greet(wall_at, span_at):
        pl.semaphore_signal(
            barrier, inc=1, device_id={"wall": wall_at, "span": span_at}, device_id_type=MESH
        )

    greet(partner, span)
    for beside in (left, right):
        greet(wall, beside)
        greet(partner, beside)

    @pl.when(has_lower)
    def _():
        greet(wall - 2, span)

    @pl.when(has_upper)
    def _():
        greet(wall + 2, span)

    own_rows = pl.ds(pl.multiple_of(rows * side, rows), rows)
    other_rows = pl.ds(pl.multiple_of(rows * (1 - side), rows), rows)
    own_mid = pl.ds(pl.multiple_of(reach + rows * side, rows), rows)
    other_mid = pl.ds(pl.multiple_of(reach + rows * (1 - side), rows), rows)
    own_top = pl.ds(pl.multiple_of(reach + pair_rows + rows * side, rows), rows)
    other_top = pl.ds(pl.multiple_of(reach + pair_rows + rows * (1 - side), rows), rows)
    own_half = pl.ds(pl.multiple_of(half * side, LANES), half)
    other_half = pl.ds(pl.multiple_of(half * (1 - side), LANES), half)
    own_cells = pl.ds(pl.multiple_of(LANES + half * side, LANES), half)
    other_cells = pl.ds(pl.multiple_of(LANES + half * (1 - side), LANES), half)
    edge_in_half = pl.ds(pl.multiple_of((half - LANES) * side, LANES), LANES)
    edge_in_full = pl.ds(pl.multiple_of(LANES + (cells - LANES) * side, LANES), LANES)
    halo_there = pl.ds(pl.multiple_of((LANES + cells) * (1 - side), LANES), LANES)
    other_edge_in_full = pl.ds(pl.multiple_of(LANES + (cells - LANES) * (1 - side), LANES), LANES)
    other_halo_there = pl.ds(pl.multiple_of((LANES + cells) * side, LANES), LANES)
    toward = (span + spans + 2 * side - 1) % spans
    away = (span + spans + 1 - 2 * side) % spans

    def parts_of(k):
        s, first, end = chunks[k]
        return s, pl.ds(first, end - first)

    def remote(source, target, send_at, recv_at, wall_at, span_at):
        return pltpu.make_async_remote_copy(
            src_ref=source, dst_ref=target, send_sem=send.at[send_at], recv_sem=recv.at[recv_at],
            device_id={"wall": wall_at, "span": span_at}, device_id_type=MESH,
        )

    def gather(k):
        at = GATHER * count + k
        s, c = parts_of(k)
        return remote(planes.at[s, c, :, other_half], ext.at[s, c, own_mid, :], at, at, partner, span)

    def up_own(k):
        at = UP_OWN * count + k
        s, c = parts_of(k)
        return remote(planes.at[s, c, :, own_half], ext.at[s, c, own_rows, :], at, at, wall + 2, span)

    def up_fwd(k):
        at = UP_FWD * count + k
        s, c = parts_of(k)
        return remote(ext.at[s, c, other_mid, :], ext.at[s, c, other_rows, :], at, at, wall + 2, span)

    def down_own(k):
        at = DOWN_OWN * count + k
        s, c = parts_of(k)
        return remote(planes.at[s, c, :, own_half], ext.at[s, c, own_top, :], at, at, wall - 2, span)

    def down_fwd(k):
        at = DOWN_FWD * count + k
        s, c = parts_of(k)
        return remote(ext.at[s, c, other_mid, :], ext.at[s, c, other_top, :], at, at, wall - 2, span)

    def give_back(k):
        at = RETURN * count + k
        s, c = parts_of(k)
        return remote(share.at[s, c], full.at[s, c, :, own_cells], at, at, partner, span)

    def own_edge(k):
        s, c = parts_of(k)
        return remote(
            full.at[s, c, :, edge_in_full], full.at[s, c, :, halo_there],
            HALO_LEFT * count + k, (HALO_LEFT + 1 - side) * count + k, wall, toward,
        )

    def other_edge(k):
        s, c = parts_of(k)
        if s < steps - 1:
            return remote(
                full.at[s, c, :, other_edge_in_full], full.at[s, c, :, other_halo_there],
                HALO_RIGHT * count + k, (HALO_LEFT + side) * count + k, wall, away,
            )
        return remote(
            share.at[s, c, :, edge_in_half], full.at[s, c, :, halo_there],
            HALO_RIGHT * count + k, (HALO_LEFT + 1 - side) * count + k, partner, toward,
        )

    def arrival(kind, k, row_at, cell_at, buffer):
        at = kind * count + k
        s, c = parts_of(k)
        target = buffer.at[s, c, row_at, cell_at]
        return remote(target, target, at, at, partner, span)

    own_in = [
        pltpu.make_async_copy(planes.at[s, :, :, own_half], ext.at[s, :, own_mid, :], local.at[s])
        for s in range(steps)
    ]
    field_in = pltpu.make_async_copy(previous, field, local.at[steps])
    width_out = pltpu.make_async_remote_copy(
        src_ref=width, dst_ref=other_width, send_sem=width_sem.at[0], recv_sem=width_sem.at[1],
        device_id={"wall": partner, "span": span}, device_id_type=MESH,
    )

    pl.semaphore_wait(barrier, 5 + has_lower.astype(jnp.int32) + has_upper.astype(jnp.int32))

    width_out.start()
    def own_out(k):
        @pl.when(has_upper)
        def _():
            up_own(k).start()

        @pl.when(has_lower)
        def _():
            down_own(k).start()

    for k in range(AHEAD):
        gather(k).start()
        own_out(k)
    for k in range(AHEAD, count):
        gather(k).start()

    field_in.start()
    for s in range(steps):
        own_in[s].start()

    @pl.when(pair == 0)
    def _():
        for s in range(steps):
            ext[s, :, 0:reach, :] = jnp.zeros((parts, reach, half), F32)

    @pl.when(pair == pairs - 1)
    def _():
        for s in range(steps):
            ext[s, :, reach + pair_rows:, :] = jnp.zeros((parts, reach, half), F32)

    tile = 2 * LANES
    depth = tile + 2 * LANES
    offset = (
        lax.broadcasted_iota(jnp.int32, (depth, tile), 0)
        - lax.broadcasted_iota(jnp.int32, (depth, tile), 1)
        - LANES
    )
    norm = math.sqrt(sum(math.exp(-2.0 * math.pi * j * j / (HZ * HZ)) ** 2 for j in range(-HZ, HZ + 1)))
    distance = offset.astype(F32)
    band = jnp.where(
        jnp.abs(offset) <= HZ, jnp.exp(distance * distance * (-2.0 * math.pi / (HZ * HZ))), 0.0
    ) * (1.0 / norm)
    head, rest = halves(band)
    span_head[...] = head
    span_rest[...] = rest

    retain_rows = jnp.exp(-math.pi / (2.0 * scale[...]))
    inject_rows = jnp.sqrt(1.0 - jnp.exp(-math.pi / scale[...]))
    retain = [columns_of(retain_rows[c:c + 1]) for c in range(parts)]
    inject = [columns_of(inject_rows[c:c + 1]) for c in range(parts)]
    factor = [columns_of(lund[i:i + 1, :]) for i in range(6)]
    drift = columns_of(mean[...])

    width_out.wait()
    depth_w = reach + pair_rows + reach
    lane = lax.broadcasted_iota(jnp.int32, (rows, 2 * depth_w), 1)
    line = lax.broadcasted_iota(jnp.int32, (rows, 2 * depth_w), 0)
    source = jnp.where(lane >= depth_w, lane - depth_w, lane)

    def wall_weights(widths, first):
        spread = columns_of(widths.astype(F32))
        apart = (source - reach - line - first).astype(F32)
        shaped = jnp.where(
            jnp.abs(apart) <= spread, jnp.exp(-2.0 * math.pi * apart * apart / (spread * spread)), 0.0
        )
        once = jnp.where(lane < depth_w, shaped * shaped, 0.0)
        return shaped / jnp.sqrt(jnp.sum(once, axis=1, keepdims=True))

    weights = jnp.concatenate(
        [wall_weights(width[...], rows * side), wall_weights(other_width[...], rows * (1 - side))], axis=0
    )
    head = weights.astype(BF16).astype(F32)
    first_copy = lax.broadcasted_iota(jnp.int32, weights.shape, 1) < depth_w
    wall_w[...] = jnp.concatenate([head, jnp.where(first_copy, weights - head, 0.0)], axis=0).astype(BF16)

    def forward(k):
        arrival(GATHER, k, other_mid, slice(None), ext).wait_recv()

        @pl.when(has_upper)
        def _():
            up_fwd(k).start()

        @pl.when(has_lower)
        def _():
            down_fwd(k).start()

        if k + AHEAD < count:
            own_out(k + AHEAD)

    def wall_pass(k):
        s, first, end = chunks[k]
        if first == 0:
            own_in[s].wait()

        @pl.when(has_lower)
        def _():
            arrival(UP_OWN, k, own_rows, slice(None), ext).wait_recv()
            arrival(UP_FWD, k, other_rows, slice(None), ext).wait_recv()

        @pl.when(has_upper)
        def _():
            arrival(DOWN_OWN, k, own_top, slice(None), ext).wait_recv()
            arrival(DOWN_FWD, k, other_top, slice(None), ext).wait_recv()

        for c in range(first, end):
            head, rest = halves(ext[s, c])
            made = jnp.dot(
                wall_w[...], jnp.concatenate([head, rest], axis=0), preferred_element_type=F32
            )
            passed = made[:pair_rows] + made[pair_rows:]
            share[s, c] = passed[rows:]
            full[s, c, :, own_cells] = passed[:rows]
        give_back(k).start()
        own_edge(k).start()
        if s == steps - 1:
            other_edge(k).start()

    def take_back(k):
        arrival(RETURN, k, slice(None), other_cells, full).wait_recv()
        if chunks[k][0] < steps - 1:
            other_edge(k).start()

    field_in.wait()
    current = [field[c] for c in range(parts)]

    def finish(s, current):
        for k in range(count):
            if chunks[k][0] == s:
                arrival(HALO_LEFT, k, slice(None), slice(0, LANES), full).wait_recv()
                arrival(HALO_RIGHT, k, slice(None), slice(LANES + cells, None), full).wait_recv()
        head, rest = halves(full[s].reshape(parts * rows, cells + 2 * LANES))
        tiles = cells // tile
        heads = jnp.concatenate([head[:, tile * t:tile * t + depth] for t in range(tiles)], axis=0)
        rests = jnp.concatenate([rest[:, tile * t:tile * t + depth] for t in range(tiles)], axis=0)
        height = heads.shape[0]
        both = jnp.dot(jnp.concatenate([heads, rests], axis=0), span_head[...], preferred_element_type=F32)
        low = jnp.dot(heads, span_rest[...], preferred_element_type=F32)
        total = both[:height] + both[height:] + low
        step = parts * rows
        filtered = jnp.concatenate([total[step * t:step * (t + 1)] for t in range(tiles)], axis=1)
        new = [
            retain[c] * current[c] + inject[c] * filtered[rows * c:rows * (c + 1)] for c in range(parts)
        ]
        velocity[s, 0] = drift + factor[0] * new[0]
        velocity[s, 1] = factor[1] * new[0] + factor[2] * new[1]
        velocity[s, 2] = factor[3] * new[0] + factor[4] * new[1] + factor[5] * new[2]
        return new

    forwarded = taken = finished = 0
    for k in range(count):
        while forwarded < min(count, LEAD + 2 * k):
            forward(forwarded)
            forwarded += 1
        wall_pass(k)
        if k > 2:
            while taken < k - 1:
                take_back(taken)
                taken += 1
            while finished < min(steps - 1, k - 2):
                current = finish(finished, current)
                finished += 1
    while taken < count:
        take_back(taken)
        taken += 1
    while finished < steps:
        current = finish(finished, current)
        finished += 1
    for c in range(parts):
        state[c] = current[c]

    for k in range(count):
        gather(k).wait_send()
        give_back(k).wait_send()
        own_edge(k).wait_send()
        other_edge(k).wait_send()

        @pl.when(has_upper)
        def _():
            up_own(k).wait_send()
            up_fwd(k).wait_send()

        @pl.when(has_lower)
        def _():
            down_own(k).wait_send()
            down_fwd(k).wait_send()


def shards(random_planes, previous, half_width, time_scale, lund_factor, mean_velocity):
    steps, parts, rows, cells = random_planes.shape
    pair_rows = 2 * rows
    assert pair_rows >= HMAX and lax.axis_size("wall") % 2 == 0
    depth = HMAX + pair_rows + HMAX
    count = len(chunks_of(steps, parts))
    hbm = pl.BlockSpec(memory_space=pltpu.HBM)
    vmem = pl.BlockSpec(memory_space=pltpu.VMEM)
    dma = pltpu.SemaphoreType.DMA
    return pl.pallas_call(
        kernel,
        out_shape=(
            jax.ShapeDtypeStruct(random_planes.shape, F32),
            jax.ShapeDtypeStruct(previous.shape, F32),
        ),
        in_specs=[hbm, hbm, vmem, vmem, vmem, vmem],
        out_specs=(vmem, vmem),
        scratch_shapes=[
            pltpu.VMEM((steps, parts, depth, cells // 2), F32),
            pltpu.VMEM((steps, parts, rows, cells // 2), F32),
            pltpu.VMEM((steps, parts, rows, cells + 2 * LANES), F32),
            pltpu.VMEM((parts, rows, cells), F32),
            pltpu.VMEM((1, rows), jnp.int32),
            pltpu.VMEM((2 * pair_rows, 2 * depth), BF16),
            pltpu.VMEM((4 * LANES, 2 * LANES), BF16),
            pltpu.VMEM((4 * LANES, 2 * LANES), BF16),
            dma((KINDS * count,)),
            dma((KINDS * count,)),
            dma((steps + 1,)),
            dma((2,)),
        ],
        compiler_params=pltpu.CompilerParams(collective_id=0, has_side_effects=True, vmem_limit_bytes=VMEM_LIMIT),
        name="inflow",
    )(*(
        pltpu.with_memory_space_constraint(array, pltpu.HBM)
        for array in (
            random_planes, previous, half_width.reshape(1, rows), time_scale, lund_factor,
            mean_velocity.reshape(1, rows),
        )
    ))


def solution(mesh):
    in_specs = (
        P(None, None, "wall", "span"),
        P(None, "wall", "span"),
        P("wall"),
        P(None, "wall"),
        P(None, "wall"),
        P("wall"),
    )
    out_specs = (P(None, None, "wall", "span"), P(None, "wall", "span"))
    return jax.shard_map(shards, mesh=mesh, in_specs=in_specs, out_specs=out_specs, check_vma=False)
```

time: 57.5 us -> 50.6 us (0.88)
  Pallas kernels: 53.3 us -> 48 us
  local copies, waits for them, and re-layouts: 3.45 us -> 1.82 us
    pallas_call x1, Pallas kernels: 53.3 us -> 48 us  [shards(): pl.pallas_call(kernel, out_shape=(jax.ShapeDtypeStruct(random_planes.shap...]
    unnamed x4 -> x2, local copies, waits for them, and re-layouts: 3.45 us -> 1.82 us
where the time goes in v2:
time: 50.6 us; the launch traced here: 50.4 us
  Pallas kernels  48 us (95%)
  local copies, waits for them, and re-layouts  1.82 us (4%)
  between operations  0.64 us (1%)
    pallas_call x1, Pallas kernels, shards(): pl.pallas_call(kernel, out_shape=(jax.ShapeDtypeStruct(random_planes.shap...  48 us
    unnamed x2, local copies, waits for them, and re-layouts  1.82 us

profile of v2, /device:TPU:0, one launch (start us, length us, event | category | flops | bytes accessed | tf_op | source)
XLA Modules:
  0.0 50.4 jit_solution(8635381582135456746)
XLA Ops:
  0.6 48.0 %inflow.1 = (f32[8,3,16,1024]{3,2,1,0:T(8,128)S(1)}, f32[3,16,1024]{2,1,0:T(8,128)S(1)}) custom-call(f32[8,3,16,1024]{3,2,1,0:T(8,128)} %planes.1, f32[3,16,1024]{2,1,0:T(8,128)} %previous.1, s32[1,16]{1,0:T(1,128)} %bitcast.2, f32[3,16]{1,0:T(4,128)} %scale.1, f32[6,16]{1,0:T(8,128)} %lund.1, f32[1,16]{1,0:T(1,128)} %bitcast.3), custom_call_target="tpu_custom_call" | custom-call | tf_op jit(solution)/shard_map/inflow/pallas_call | solution.py:374
  48.6 1.1 %copy.10 = f32[8,3,16,1024]{3,2,1,0:T(8,128)} copy(f32[8,3,16,1024]{3,2,1,0:T(8,128)S(1)} %get-tuple-element.4) | data formatting | bytes 3145728
  49.7 0.7 %copy.11 = f32[3,16,1024]{2,1,0:T(8,128)} copy(f32[3,16,1024]{2,1,0:T(8,128)S(1)} %get-tuple-element.5) | data formatting | bytes 393216

commit v3 on v2

--- a/solution.py
+++ b/solution.py
@@ -38,9 +38,9 @@
 
 
 def kernel(
-    planes, previous, width, scale, lund, mean, velocity, state,
-    ext, share, full, field, other_width, wall_w, span_head, span_rest,
-    send, recv, local, width_sem,
+    planes, previous, width_hbm, scale_hbm, lund_hbm, mean_hbm, velocity, state,
+    ext, share, full, field, width, scale, lund, mean, other_width, wall_w, span_head, span_rest,
+    send, recv, local, small, width_sem,
 ):
     steps, parts, rows, cells = planes.shape
     chunks = chunks_of(steps, parts)
@@ -168,8 +168,14 @@
         for s in range(steps)
     ]
     field_in = pltpu.make_async_copy(previous, field, local.at[steps])
+    small_in = [
+        pltpu.make_async_copy(source, target, small.at[i])
+        for i, (source, target) in enumerate(
+            ((width_hbm, width), (scale_hbm, scale), (lund_hbm, lund), (mean_hbm, mean))
+        )
+    ]
     width_out = pltpu.make_async_remote_copy(
-        src_ref=width, dst_ref=other_width, send_sem=width_sem.at[0], recv_sem=width_sem.at[1],
+        src_ref=width_hbm, dst_ref=other_width, send_sem=width_sem.at[0], recv_sem=width_sem.at[1],
         device_id={"wall": partner, "span": span}, device_id_type=MESH,
     )
 
@@ -191,6 +197,8 @@
     for k in range(AHEAD, count):
         gather(k).start()
 
+    for copy in small_in:
+        copy.start()
     field_in.start()
     for s in range(steps):
         own_in[s].start()
@@ -221,6 +229,8 @@
     span_head[...] = head
     span_rest[...] = rest
 
+    for copy in small_in:
+        copy.wait()
     retain_rows = jnp.exp(-math.pi / (2.0 * scale[...]))
     inject_rows = jnp.sqrt(1.0 - jnp.exp(-math.pi / scale[...]))
     retain = [columns_of(retain_rows[c:c + 1]) for c in range(parts)]
@@ -362,6 +372,17 @@
             down_fwd(k).wait_send()
 
 
+def put_out(*refs):
+    half = len(refs) // 2
+    copies = [
+        pltpu.make_async_copy(refs[i], refs[half + i], refs[-1].at[i]) for i in range(2)
+    ]
+    for copy in copies:
+        copy.start()
+    for copy in copies:
+        copy.wait()
+
+
 def shards(random_planes, previous, half_width, time_scale, lund_factor, mean_velocity):
     steps, parts, rows, cells = random_planes.shape
     pair_rows = 2 * rows
@@ -371,13 +392,13 @@
     hbm = pl.BlockSpec(memory_space=pltpu.HBM)
     vmem = pl.BlockSpec(memory_space=pltpu.VMEM)
     dma = pltpu.SemaphoreType.DMA
-    return pl.pallas_call(
+    results = pl.pallas_call(
         kernel,
         out_shape=(
             jax.ShapeDtypeStruct(random_planes.shape, F32),
             jax.ShapeDtypeStruct(previous.shape, F32),
         ),
-        in_specs=[hbm, hbm, vmem, vmem, vmem, vmem],
+        in_specs=[hbm] * 6,
         out_specs=(vmem, vmem),
         scratch_shapes=[
             pltpu.VMEM((steps, parts, depth, cells // 2), F32),
@@ -385,12 +406,17 @@
             pltpu.VMEM((steps, parts, rows, cells + 2 * LANES), F32),
             pltpu.VMEM((parts, rows, cells), F32),
             pltpu.VMEM((1, rows), jnp.int32),
+            pltpu.VMEM(time_scale.shape, F32),
+            pltpu.VMEM(lund_factor.shape, F32),
+            pltpu.VMEM((1, rows), F32),
+            pltpu.VMEM((1, rows), jnp.int32),
             pltpu.VMEM((2 * pair_rows, 2 * depth), BF16),
             pltpu.VMEM((4 * LANES, 2 * LANES), BF16),
             pltpu.VMEM((4 * LANES, 2 * LANES), BF16),
             dma((KINDS * count,)),
             dma((KINDS * count,)),
             dma((steps + 1,)),
+            dma((4,)),
             dma((2,)),
         ],
         compiler_params=pltpu.CompilerParams(collective_id=0, has_side_effects=True, vmem_limit_bytes=VMEM_LIMIT),
@@ -402,6 +428,16 @@
             mean_velocity.reshape(1, rows),
         )
     ))
+    space = pl.BlockSpec(memory_space=pl.ANY)
+    return pl.pallas_call(
+        put_out,
+        out_shape=tuple(jax.ShapeDtypeStruct(r.shape, r.dtype) for r in results),
+        in_specs=[space] * 2,
+        out_specs=(hbm, hbm),
+        scratch_shapes=[dma((2,))],
+        compiler_params=pltpu.CompilerParams(vmem_limit_bytes=VMEM_LIMIT),
+        name="put_out",
+    )(*results)
 
 
 def solution(mesh):

time: 50.6 us -> 49.3 us (0.974)
  local copies, waits for them, and re-layouts: 1.82 us -> 0 us
  Pallas kernels: 48 us -> 48.6 us
    unnamed x2 -> x0, local copies, waits for them, and re-layouts: 1.82 us -> none
    pallas_call x0 -> x1, Pallas kernels: none -> 1.21 us  [shards(): pl.pallas_call(put_out, out_shape=tuple((jax.ShapeDtypeStruct(r.shape, r....]
    pallas_call x1, Pallas kernels: 48 us -> 47.3 us  [shards(): pl.pallas_call(kernel, out_shape=(jax.ShapeDtypeStruct(random_planes.shap...]
where the time goes in v3:
time: 49.3 us; the launch traced here: 49.2 us
  Pallas kernels  48.6 us (99%)
  between operations  0.64 us (1%)
    pallas_call x1, Pallas kernels, shards(): pl.pallas_call(kernel, out_shape=(jax.ShapeDtypeStruct(random_planes.shap...  47.3 us
    pallas_call x1, Pallas kernels, shards(): pl.pallas_call(put_out, out_shape=tuple((jax.ShapeDtypeStruct(r.shape, r....  1.21 us

profile of v3, /device:TPU:0, one launch (start us, length us, event | category | flops | bytes accessed | tf_op | source)
XLA Modules:
  0.0 49.2 jit_solution(11320154500944723809)
XLA Ops:
  0.6 47.3 %inflow.1 = (f32[8,3,16,1024]{3,2,1,0:T(8,128)S(1)}, f32[3,16,1024]{2,1,0:T(8,128)S(1)}) custom-call(f32[8,3,16,1024]{3,2,1,0:T(8,128)} %planes.1, f32[3,16,1024]{2,1,0:T(8,128)} %previous.1, s32[1,16]{1,0:T(1,128)} %bitcast.2, f32[3,16]{1,0:T(4,128)} %scale_hbm.1, f32[6,16]{1,0:T(8,128)} %lund_hbm.1, f32[1,16]{1,0:T(1,128)} %bitcast.3), custom_call_target="tpu_custom_call" | custom-call | tf_op jit(solution)/shard_map/inflow/pallas_call | solution.py:395
  48.0 1.2 %put_out.1 = (f32[8,3,16,1024]{3,2,1,0:T(8,128)}, f32[3,16,1024]{2,1,0:T(8,128)}) custom-call(f32[8,3,16,1024]{3,2,1,0:T(8,128)S(1)} %get-tuple-element.4.refs_0_, f32[3,16,1024]{2,1,0:T(8,128)S(1)} %get-tuple-element.5.refs_1_), custom_call_target="tpu_custom_call" | custom-call | tf_op jit(solution)/shard_map/put_out/pallas_call | solution.py:432
